TPU v7x, 32 devices: a whole 2x2x4 slice. The times are simulated.
32 devices in a mesh: tm: 4 (over y, core), space: 8 (over z, x).
Axes of the slice: x: 2, y: 2, z: 4, core: 2. Of those that a mesh axis runs over, the one named last changes fastest.
Arguments:
- observed: float32 [8, 48, 1440], P('tm', 'space'), may hold values from -8 to 8
- noise_var: float32 [8], replicated, may hold values from 0.05 to 1
- spectral_var: float32 [1440, 48], P('space'), may hold values from 0.2 to 5
- time_scale: float32 [1440, 48], P('space'), may hold values from 1.5 to 2
Outputs:
- smoothed: float32 [8, 48, 1440], P('tm', 'space')
All inputs are finite; a program needn't handle non-finite values.
Results may differ from a plain program's by a relative error of at most 0.00007.
Values sent between devices are 32-bit elements; how exact they have to be, the bound alone decides.
A program may use at most 64 MiB of HBM per device.

v0:
```python
import math

import jax
import jax.numpy as jnp
from jax import lax
from jax.sharding import PartitionSpec as P

HIGHEST = lax.Precision.HIGHEST
ROOT_FIVE = 2.23606797749979
NILPOTENT = ((1.0, 1.0, 0.0), (0.0, 1.0, 1.0), (-1.0, -3.0, -2.0))
NILPOTENT_SQUARED = ((1.0, 2.0, 1.0), (-1.0, -2.0, -1.0), (1.0, 2.0, 1.0))
STATIONARY = ((1.0, 0.0, -1.0 / 3.0), (0.0, 1.0 / 3.0, 0.0), (-1.0 / 3.0, 0.0, 1.0))


def lon_basis(size):
    mode_index = lax.broadcasted_iota(jnp.int32, (size, size), 0)
    longitude = lax.broadcasted_iota(jnp.int32, (size, size), 1)
    half_size = size // 2
    sine_rows = mode_index > half_size
    frequency = jnp.where(sine_rows, mode_index - half_size, mode_index)
    radians = (frequency * longitude % size).astype(jnp.float32) * (2.0 * math.pi / size)
    waveform = jnp.where(sine_rows, jnp.sin(radians), jnp.cos(radians))
    edge_rows = (mode_index == 0) | (mode_index == half_size)
    weight = jnp.where(edge_rows, math.sqrt(1.0 / size), math.sqrt(2.0 / size))
    return waveform * weight


def lat_basis(size):
    wavenumber = lax.broadcasted_iota(jnp.int32, (size, size), 0)
    latitude = lax.broadcasted_iota(jnp.int32, (size, size), 1)
    radians = (wavenumber * (2 * latitude + 1) % (4 * size)).astype(jnp.float32) * (
        math.pi / (2.0 * size)
    )
    weight = jnp.where(wavenumber == 0, math.sqrt(1.0 / size), math.sqrt(2.0 / size))
    return jnp.cos(radians) * weight


def mat_mul(left, right):
    return [
        [
            left[across][0] * right[0][within]
            + left[across][1] * right[1][within]
            + left[across][2] * right[2][within]
            for within in range(3)
        ]
        for across in range(3)
    ]


def mat_vec(matrix, vector):
    return [
        matrix[across][0] * vector[0]
        + matrix[across][1] * vector[1]
        + matrix[across][2] * vector[2]
        for across in range(3)
    ]


def transposed(matrix):
    return [[matrix[within][across] for within in range(3)] for across in range(3)]


def inverted(matrix):
    cofactor = [
        [
            matrix[1][1] * matrix[2][2] - matrix[1][2] * matrix[2][1],
            matrix[0][2] * matrix[2][1] - matrix[0][1] * matrix[2][2],
            matrix[0][1] * matrix[1][2] - matrix[0][2] * matrix[1][1],
        ],
        [
            matrix[1][2] * matrix[2][0] - matrix[1][0] * matrix[2][2],
            matrix[0][0] * matrix[2][2] - matrix[0][2] * matrix[2][0],
            matrix[0][2] * matrix[1][0] - matrix[0][0] * matrix[1][2],
        ],
        [
            matrix[1][0] * matrix[2][1] - matrix[1][1] * matrix[2][0],
            matrix[0][1] * matrix[2][0] - matrix[0][0] * matrix[2][1],
            matrix[0][0] * matrix[1][1] - matrix[0][1] * matrix[1][0],
        ],
    ]
    determinant = (
        matrix[0][0] * cofactor[0][0]
        + matrix[0][1] * cofactor[1][0]
        + matrix[0][2] * cofactor[2][0]
    )
    return [[cofactor[across][within] / determinant for within in range(3)] for across in range(3)]


def model_terms(variance, scale):
    decay_rate = ROOT_FIVE / scale
    damping = jnp.exp(-decay_rate)
    transition = [
        [
            damping
            * (
                (1.0 if across == within else 0.0)
                + decay_rate * NILPOTENT[across][within]
                + 0.5 * decay_rate * decay_rate * NILPOTENT_SQUARED[across][within]
            )
            for within in range(3)
        ]
        for across in range(3)
    ]
    stationary = [
        [variance * STATIONARY[across][within] for within in range(3)] for across in range(3)
    ]
    carried = mat_mul(mat_mul(transition, stationary), transposed(transition))
    process_noise = [
        [stationary[across][within] - carried[across][within] for within in range(3)]
        for across in range(3)
    ]
    return (transition, stationary, process_noise)


def predict_cov(covariance, transition, process_noise):
    carried = mat_mul(mat_mul(transition, covariance), transposed(transition))
    return [
        [carried[across][within] + process_noise[across][within] for within in range(3)]
        for across in range(3)
    ]


def gain_and_cov(predicted_cov, noise):
    innovation_var = predicted_cov[0][0] + noise
    kalman_gain = [predicted_cov[across][0] / innovation_var for across in range(3)]
    covariance = [
        [
            predicted_cov[across][within] - kalman_gain[across] * predicted_cov[0][within]
            for within in range(3)
        ]
        for across in range(3)
    ]
    return (kalman_gain, covariance)


def smooth_series(spectra, noise_var, variance, scale):
    transition, stationary, process_noise = model_terms(variance, scale)
    zeros = jnp.zeros_like(variance)

    def forward(carry, inputs):
        mean_state, covariance = carry
        observed, noise = inputs
        predicted_cov = predict_cov(covariance, transition, process_noise)
        smoother_gain = mat_mul(
            mat_mul(covariance, transposed(transition)), inverted(predicted_cov)
        )
        predicted = mat_vec(transition, mean_state)
        kalman_gain, covariance = gain_and_cov(predicted_cov, noise)
        residual = observed - predicted[0]
        mean_state = [predicted[across] + kalman_gain[across] * residual for across in range(3)]
        return ((mean_state, covariance), (mean_state, smoother_gain))

    _, (means, gains) = lax.scan(forward, ([zeros, zeros, zeros], stationary), (spectra, noise_var))

    def backward(later, inputs):
        mean_state, smoother_gain = inputs
        projected = mat_vec(transition, mean_state)
        difference = [later[across] - projected[across] for across in range(3)]
        correction = mat_vec(smoother_gain, difference)
        smoothed_state = [mean_state[across] + correction[across] for across in range(3)]
        return (smoothed_state, smoothed_state[0])

    last_state = [means[across][-1] for across in range(3)]
    earlier_means = [means[across][:-1] for across in range(3)]
    next_gains = [[gains[across][within][1:] for within in range(3)] for across in range(3)]
    _, field = lax.scan(backward, last_state, (earlier_means, next_gains), reverse=True)
    return jnp.concatenate([field, last_state[0][None]], axis=0)


def per_device(observed, noise_var, spectral_var, time_scale):
    hours_dev, lat_dev, lon_size = observed.shape
    band_count = lax.axis_size("space")
    lat_size = lat_dev * band_count
    modes_dev = lon_size // band_count
    lon_table = lon_basis(lon_size)
    lat_table = lat_basis(lat_size).reshape(lat_size, band_count, lat_dev)
    grid_rows = observed.reshape(hours_dev * lat_dev, lon_size)
    spectra = lax.dot_general(lon_table, grid_rows, (((1,), (1,)), ((), ())), precision=HIGHEST)
    by_mode = lax.all_to_all(spectra, "space", split_axis=0, concat_axis=1, tiled=True)
    by_mode = by_mode.reshape(modes_dev, band_count, hours_dev, lat_dev)
    coefficients = jnp.einsum("msha,nsa->hmn", by_mode, lat_table, precision=HIGHEST)
    flat = coefficients.reshape(hours_dev, modes_dev * lat_size)
    hourly = lax.all_to_all(flat, "tm", split_axis=1, concat_axis=0, tiled=True)
    share = flat.shape[1] // lax.axis_size("tm")
    offset = lax.axis_index("tm") * share
    variance = lax.dynamic_slice_in_dim(spectral_var.reshape(-1), offset, share)
    scale = lax.dynamic_slice_in_dim(time_scale.reshape(-1), offset, share)
    series = smooth_series(hourly, noise_var, variance, scale)
    smooth = lax.all_to_all(series, "tm", split_axis=0, concat_axis=1, tiled=True).reshape(
        hours_dev, modes_dev, lat_size
    )
    latitude_grid = jnp.einsum("hmn,nsa->msha", smooth, lat_table, precision=HIGHEST)
    latitude_grid = latitude_grid.reshape(modes_dev, band_count * hours_dev * lat_dev)
    by_band = lax.all_to_all(latitude_grid, "space", split_axis=1, concat_axis=0, tiled=True)
    field = lax.dot_general(by_band, lon_table, (((0,), (0,)), ((), ())), precision=HIGHEST)
    return field.reshape(hours_dev, lat_dev, lon_size)


def solution(mesh):
    placed = (P("tm", "space", None), P(), P("space", None), P("space", None))
    return jax.shard_map(
        per_device, mesh=mesh, in_specs=placed, out_specs=P("tm", "space", None), check_vma=False
    )
```

profile of v0, /device:TPU:0, one launch (start us, length us, event | category | flops | bytes accessed | tf_op | source)
XLA Modules:
  0.0 186.0 jit_solution(13239352672636849324)
XLA Ops:
  0.0 0.9 copy.39
  1.0 39.0 %fusion.103 = f32[8,180,1440]{2,1,0:T(8,128)S(1)} fusion(f32[8,180]{1,0:T(8,128)S(1)} %fusion.79, s32[8,180]{1,0:T(8,128)S(1)} %get-tuple-element.1149, s32[8,180]{1,0:T(8,128)S(1)} %get-tuple-element.1150, pred[8,180]{1,0:T(8,128)(4,1)S(1)} %fusion.77), kind=kLoop, calls=%fused_computation.86.clone.1 | loop fusion | flops 24883200 | bytes 8313120 | tf_op jit(solution)/shard_map/dot_general | solution.py:178
  40.0 8.4 %fusion.2 = f32[8,180,12]{1,2,0:T(8,128)} fusion(f32[12,1440,1]{1,0,2:T(8,128)S(1)} %reshape.200, f32[8,180,1440]{2,1,0:T(8,128)S(1)} %fusion.103), kind=kOutput, calls=%fused_computation.85 | convolution fusion | flops 298598400 | bytes 8432640 | tf_op jit(solution)/shard_map/dot_general | solution.py:178
  48.4 7.3 %all-to-all-start = ((f32[8,180,12]{1,2,0:T(8,128)}), f32[8,180,12]{1,2,0:T(8,128)S(1)}, u32[]{:S(2)}, u32[]{:S(2)}) async-start(f32[8,180,12]{1,2,0:T(8,128)} %fusion.2), calls=%async_computation | async-start | bytes 262144 | tf_op jit(solution)/shard_map/all_to_all | solution.py:179
  56.2 6.8 %all-to-all-done = f32[8,180,12]{1,2,0:T(8,128)S(1)} async-done(((f32[8,180,12]{1,2,0:T(8,128)}), f32[8,180,12]{1,2,0:T(8,128)S(1)}, u32[]{:S(2)}, u32[]{:S(2)}) %all-to-all-start) | async-done | bytes 69152 | tf_op jit(solution)/shard_map/all_to_all | solution.py:179
  64.4 3.3 %all-to-all-start.1 = ((f32[2,4,2160]{2,0,1:T(2,128)}), f32[2,4,2160]{2,0,1:T(2,128)S(1)}, u32[]{:S(2)}, u32[]{:S(2)}) async-start(f32[2,4,2160]{2,0,1:T(2,128)} %copy.42), calls=%async_computation.1 | async-start | bytes 139264 | tf_op jit(solution)/shard_map/all_to_all | solution.py:183
  68.1 3.8 %all-to-all-done.1 = f32[2,4,2160]{2,0,1:T(2,128)S(1)} async-done(((f32[2,4,2160]{2,0,1:T(2,128)}), f32[2,4,2160]{2,0,1:T(2,128)S(1)}, u32[]{:S(2)}, u32[]{:S(2)}) %all-to-all-start.1) | async-done | bytes 69152 | tf_op jit(solution)/shard_map/all_to_all | solution.py:183
  71.9 40.9 %while.78 = (s32[]{:T(128)}, f32[2160]{0:T(1024)S(1)}, f32[2160]{0:T(1024)S(1)}, f32[2160]{0:T(1024)S(1)}, f32[2160]{0:T(1024)S(1)}, /*index=5*/f32[2160]{0:T(10...) while((s32[]{:T(128)}, f32[2160]{0:T(1024)S(1)}, ...), condition=%wide.region_1.2_spmd.clone, body=%wide.region_0.1_spmd.clone.sunk | while | flops 611283 | bytes 2022240 | solution.py:153
  74.9 0.7 multiply_subtract_fusion.16
  80.0 0.7 multiply_subtract_fusion.16
  85.1 0.7 multiply_subtract_fusion.16
  90.2 0.7 multiply_subtract_fusion.16
  95.3 0.7 multiply_subtract_fusion.16
  100.4 0.7 multiply_subtract_fusion.16
  105.6 0.7 multiply_subtract_fusion.16
  110.7 0.7 multiply_subtract_fusion.16
  113.1 5.0 %while.77 = (s32[]{:T(128)}, f32[2160]{0:T(1024)S(1)}, f32[2160]{0:T(1024)S(1)}, f32[2160]{0:T(1024)S(1)}, f32[7,2160]{1,0:T(8,128)S(1)}, /*index=5*/f32[7,2160]...) while((s32[]{:T(128)}, f32[2160]{0:T(1024)S(1)}, ...), condition=%wide.region_3.4_spmd, body=%wide.region_2.3_spmd.sunk | while | flops 77763 | bytes 544613 | solution.py:166
  118.1 0.7 all_to_all.56
  118.8 3.3 %all-to-all-start.2 = ((f32[4,2,2160]{2,1,0:T(2,128)}), f32[4,2,2160]{2,1,0:T(2,128)S(1)}, u32[]{:S(2)}, u32[]{:S(2)}) async-start(f32[4,2,2160]{2,1,0:T(2,128)} %all_to_all.56), calls=%async_computation.2 | async-start | bytes 139264 | tf_op jit(solution)/shard_map/all_to_all | solution.py:189
  122.1 4.1 %all-to-all-done.2 = f32[4,2,2160]{2,1,0:T(2,128)S(1)} async-done(((f32[4,2,2160]{2,1,0:T(2,128)}), f32[4,2,2160]{2,1,0:T(2,128)S(1)}, u32[]{:S(2)}, u32[]{:S(2)}) %all-to-all-start.2) | async-done | bytes 69152 | tf_op jit(solution)/shard_map/all_to_all | solution.py:189
  127.6 3.6 %all-to-all-start.3 = ((f32[180,8,12]{0,2,1:T(8,128)}), f32[180,8,12]{0,2,1:T(8,128)S(1)}, u32[]{:S(2)}, u32[]{:S(2)}) async-start(f32[180,8,12]{0,2,1:T(8,128)} %copy.46), calls=%async_computation.3 | async-start | bytes 262144 | tf_op jit(solution)/shard_map/all_to_all | solution.py:194
  131.3 7.0 %all-to-all-done.3 = f32[180,8,12]{0,2,1:T(8,128)S(1)} async-done(((f32[180,8,12]{0,2,1:T(8,128)}), f32[180,8,12]{0,2,1:T(8,128)S(1)}, u32[]{:S(2)}, u32[]{:S(2)}) %all-to-all-start.3) | async-done | bytes 69152 | tf_op jit(solution)/shard_map/all_to_all | solution.py:194
  138.5 46.8 %fusion.15 = f32[2,6,1440]{2,1,0:T(8,128)S(1)} fusion(f32[2,6,1440]{2,1,0:T(8,128)S(1)} %dot_general.20, f32[1440]{0:T(1024)S(1)} %fusion.81, s32[1440]{0:T(1024)S(1)} %iota_add_fusion, pred[1440]{0:T(1024)(128)(4,1)S(1)} %iota_compare_fusion.2), kind=kOutput, calls=%fused_computation.97 | convolution fusion | flops 323481600 | bytes 151200 | tf_op jit(solution)/shard_map/dot_general | solution.py:195
  185.3 0.7 copy.48
  (403 shorter events, 41.8 us)
Async XLA Ops:
  1.0 54.7 %copy-start = (f32[180,48]{0,1:T(8,128)S(1)}, f32[180,48]{0,1:T(8,128)}, u32[]{:S(2)}) copy-start(f32[180,48]{0,1:T(8,128)} %param.11) | copy-start | bytes 103684
  1.0 54.9 %copy-start.1 = (f32[180,48]{0,1:T(8,128)S(1)}, f32[180,48]{0,1:T(8,128)}, u32[]{:S(2)}) copy-start(f32[180,48]{0,1:T(8,128)} %param.10) | copy-start | bytes 103684
  1.0 70.9 %copy-start.2 = (f32[8]{0:T(128)S(1)}, f32[8]{0:T(128)}, u32[]{:S(2)}) copy-start(f32[8]{0:T(128)} %param.9) | copy-start | bytes 100
  48.4 14.6 %all-to-all-start = ((f32[8,180,12]{1,2,0:T(8,128)}), f32[8,180,12]{1,2,0:T(8,128)S(1)}, u32[]{:S(2)}, u32[]{:S(2)}) async-start(f32[8,180,12]{1,2,0:T(8,128)} %fusion.2), calls=%async_computation | async-start | bytes 262144 | tf_op jit(solution)/shard_map/all_to_all | solution.py:179
  64.4 7.4 %all-to-all-start.1 = ((f32[2,4,2160]{2,0,1:T(2,128)}), f32[2,4,2160]{2,0,1:T(2,128)S(1)}, u32[]{:S(2)}, u32[]{:S(2)}) async-start(f32[2,4,2160]{2,0,1:T(2,128)} %copy.42), calls=%async_computation.1 | async-start | bytes 139264 | tf_op jit(solution)/shard_map/all_to_all | solution.py:183
  118.8 7.4 %all-to-all-start.2 = ((f32[4,2,2160]{2,1,0:T(2,128)}), f32[4,2,2160]{2,1,0:T(2,128)S(1)}, u32[]{:S(2)}, u32[]{:S(2)}) async-start(f32[4,2,2160]{2,1,0:T(2,128)} %all_to_all.56), calls=%async_computation.2 | async-start | bytes 139264 | tf_op jit(solution)/shard_map/all_to_all | solution.py:189
  127.6 10.7 %all-to-all-start.3 = ((f32[180,8,12]{0,2,1:T(8,128)}), f32[180,8,12]{0,2,1:T(8,128)S(1)}, u32[]{:S(2)}, u32[]{:S(2)}) async-start(f32[180,8,12]{0,2,1:T(8,128)} %copy.46), calls=%async_computation.3 | async-start | bytes 262144 | tf_op jit(solution)/shard_map/all_to_all | solution.py:194
where the time goes:
time: 187 us; the launch traced here: 186 us
  matrix products  56.3 us (30%)
  other arithmetic  52 us (28%)
  local copies, waits for them, and re-layouts  35.5 us (19%)
  waiting for transfers between devices  21.7 us (12%)
  starting transfers between devices  17.4 us (9%)
  loops' own time  2.67 us (1%)
    dot_general x1, matrix products, per_device(): lax.dot_general(by_band, lon_table, (((0,), (0,)), ((), ())), precision=H...  46.8 us
    dot_general x1, other arithmetic, per_device(): lax.dot_general(lon_table, grid_rows, (((1,), (1,)), ((), ())), precision...  39 us
    dynamic_update_slice x96, local copies, waits for them, and re-layouts, smooth_series(): lax.scan(forward, ([zeros, zeros, zeros], stationary), (spectra, noise_var))  20.7 us
    dot_general x1, matrix products, per_device(): lax.dot_general(lon_table, grid_rows, (((1,), (1,)), ((), ())), precision...  8.38 us
    all_to_all x1, starting transfers between devices, per_device(): lax.all_to_all(spectra, 'space', split_axis=0, concat_axis=1, tiled=True)  7.28 us
    all_to_all x1, waiting for transfers between devices, per_device(): lax.all_to_all(latitude_grid, 'space', split_axis=1, concat_axis=0, tiled...  7.04 us
    all_to_all x1, waiting for transfers between devices, per_device(): lax.all_to_all(spectra, 'space', split_axis=0, concat_axis=1, tiled=True)  6.77 us
    sub x8, other arithmetic, gain_and_cov(): predicted_cov[across][within]  5.43 us
  transfers between devices with their start and end apart: 4, of which 4 were waited for; matrix products, arithmetic and copies ran while one was open for 0% of the time, Pallas kernels for 0%

commit v1 on v0

--- a/solution.py
+++ b/solution.py
@@ -1,8 +1,12 @@
+import functools
 import math
 
 import jax
 import jax.numpy as jnp
+import numpy as np
 from jax import lax
+from jax.experimental import pallas as pl
+from jax.experimental.pallas import tpu as pltpu
 from jax.sharding import PartitionSpec as P
 
 HIGHEST = lax.Precision.HIGHEST
@@ -167,7 +171,7 @@
     return jnp.concatenate([field, last_state[0][None]], axis=0)
 
 
-def per_device(observed, noise_var, spectral_var, time_scale):
+def per_device_general(observed, noise_var, spectral_var, time_scale):
     hours_dev, lat_dev, lon_size = observed.shape
     band_count = lax.axis_size("space")
     lat_size = lat_dev * band_count
@@ -196,6 +200,397 @@
     return field.reshape(hours_dev, lat_dev, lon_size)
 
 
+LANES = 128
+ROWS = 8
+MESH = pl.DeviceIdType.MESH
+NT = (((1,), (1,)), ((), ()))
+NN = (((1,), (0,)), ((), ()))
+
+
+def round_up(value, unit):
+    return -(-value // unit) * unit
+
+
+def lon_tables(lon_size, times, bands, slots_used):
+    half = lon_size // 2
+    modes_dev = lon_size // bands
+    slots = modes_dev // times
+    mode = (
+        np.arange(bands)[None, :, None] * modes_dev
+        + np.arange(times)[:, None, None]
+        + times * np.arange(slots)[None, None, :]
+    )
+    sine = mode > half
+    frequency = np.where(sine, mode - half, mode)
+    radians = (frequency[..., None] * np.arange(half) % lon_size) * (2.0 * math.pi / lon_size)
+    waveform = np.where(sine[..., None], np.sin(radians), np.cos(radians))
+    edge = (mode == 0) | (mode == half)
+    table = waveform * np.where(edge, math.sqrt(1.0 / lon_size), math.sqrt(2.0 / lon_size))[..., None]
+    full = np.zeros((times, bands, slots_used, round_up(half, LANES)), np.float32)
+    full[:, :, :slots, :half] = table
+    high = full.astype(jnp.bfloat16)
+    low = (full - high.astype(np.float32)).astype(jnp.bfloat16)
+    return high, low
+
+
+def lat_tables(lat_size, bands):
+    lat_dev = lat_size // bands
+    wavenumber = np.arange(lat_size)[:, None]
+    latitude = np.arange(lat_size)[None, :]
+    radians = (wavenumber * (2 * latitude + 1) % (4 * lat_size)) * (math.pi / (2.0 * lat_size))
+    table = np.cos(radians) * np.where(wavenumber == 0, math.sqrt(1.0 / lat_size), math.sqrt(2.0 / lat_size))
+    full = np.zeros((lat_size, bands, ROWS), np.float32)
+    full[:, :, :lat_dev] = table.reshape(lat_size, bands, lat_dev)
+    full = full.reshape(lat_size, bands * ROWS)
+    return full, np.ascontiguousarray(full.T)
+
+
+def split(value):
+    high = value.astype(jnp.bfloat16)
+    low = (value - high.astype(jnp.float32)).astype(jnp.bfloat16)
+    return high, low
+
+
+def swap_halves(first, second):
+    left = lax.broadcasted_iota(jnp.int32, first.shape, 1) < LANES // 2
+    return (
+        jnp.where(left, first, pltpu.roll(second, LANES // 2, 1)),
+        jnp.where(left, pltpu.roll(first, LANES // 2, 1), second),
+    )
+
+
+def symmetric_gains(noise_ref, variance, scale, transition_ref, gain_ref, smoother_ref):
+    hours = gain_ref.shape[0]
+    transition, stationary, process = model_terms(variance, scale)
+    pairs = [(0, 0), (0, 1), (0, 2), (1, 1), (1, 2), (2, 2)]
+    for row in range(3):
+        for column in range(3):
+            transition_ref[row, column] = transition[row][column]
+
+    def unpack(packed):
+        matrix = [[None] * 3 for _ in range(3)]
+        for (row, column), value in zip(pairs, packed):
+            matrix[row][column] = matrix[column][row] = value
+        return matrix
+
+    def update(predicted, hour):
+        inverse_var = 1.0 / (predicted[0][0] + noise_ref[hour])
+        gain = [predicted[row][0] * inverse_var for row in range(3)]
+        for row in range(3):
+            gain_ref[hour, row] = gain[row]
+        return [predicted[row][column] - gain[row] * predicted[0][column] for row, column in pairs]
+
+    def step(hour, packed):
+        covariance = unpack(packed)
+        moved = mat_mul(transition, covariance)
+        predicted = unpack(
+            [
+                moved[row][0] * transition[column][0]
+                + moved[row][1] * transition[column][1]
+                + moved[row][2] * transition[column][2]
+                + process[row][column]
+                for row, column in pairs
+            ]
+        )
+        c00 = predicted[1][1] * predicted[2][2] - predicted[1][2] * predicted[1][2]
+        c01 = predicted[0][2] * predicted[1][2] - predicted[0][1] * predicted[2][2]
+        c02 = predicted[0][1] * predicted[1][2] - predicted[0][2] * predicted[1][1]
+        c11 = predicted[0][0] * predicted[2][2] - predicted[0][2] * predicted[0][2]
+        c12 = predicted[0][1] * predicted[0][2] - predicted[0][0] * predicted[1][2]
+        c22 = predicted[0][0] * predicted[1][1] - predicted[0][1] * predicted[0][1]
+        inverse_det = 1.0 / (predicted[0][0] * c00 + predicted[0][1] * c01 + predicted[0][2] * c02)
+        cofactors = unpack([c00, c01, c02, c11, c12, c22])
+        for row in range(3):
+            scaled = [moved[within][row] * inverse_det for within in range(3)]
+            for column in range(3):
+                smoother_ref[hour - 1, row, column] = (
+                    scaled[0] * cofactors[0][column]
+                    + scaled[1] * cofactors[1][column]
+                    + scaled[2] * cofactors[2][column]
+                )
+        return tuple(update(predicted, hour))
+
+    first = tuple(update(stationary, 0))
+    lax.fori_loop(1, hours, step, first)
+
+
+def smoother_kernel(
+    times,
+    bands,
+    slots_used,
+    observed_ref,
+    noise_ref,
+    variance_ref,
+    scale_ref,
+    forward_lat_ref,
+    inverse_lat_ref,
+    high_hbm,
+    low_hbm,
+    out_ref,
+    high,
+    low,
+    folded,
+    outbox,
+    inbox,
+    outbox_back,
+    inbox_back,
+    transition_ref,
+    gain_ref,
+    smoother_ref,
+    table_sem,
+    send_sem,
+    recv_sem,
+    send_back_sem,
+    recv_back_sem,
+):
+    devices = times * bands
+    my_time = lax.axis_index("tm")
+    my_band = lax.axis_index("space")
+    me = my_time * bands + my_band
+    lat_dev, lon_size = observed_ref.shape[1], observed_ref.shape[2]
+    half = lon_size // 2
+    hours = gain_ref.shape[0]
+    n_half = gain_ref.shape[2]
+    width = LANES // 2
+
+    def table_copy(time, which):
+        source, target = ((high_hbm, high), (low_hbm, low))[which]
+        return pltpu.make_async_copy(
+            source.at[time], target.at[time, :, pl.ds(0, slots_used), :], table_sem.at[time, which]
+        )
+
+    for time in range(times):
+        table_copy(time, 0).start()
+        table_copy(time, 1).start()
+
+    inbox[...] = jnp.zeros_like(inbox)
+    inbox_back[...] = jnp.zeros_like(inbox_back)
+
+    barrier = pltpu.get_barrier_semaphore()
+
+    def greet(step, carry):
+        peer = lax.rem(me + step, devices)
+        pl.semaphore_signal(
+            barrier, inc=1, device_id=(peer // bands, lax.rem(peer, bands)), device_id_type=MESH
+        )
+        return carry
+
+    lax.fori_loop(1, devices, greet, 0)
+
+    spare = width - slots_used
+    high[:, :, slots_used:, :] = jnp.zeros((times, bands, spare, high.shape[3]), high.dtype)
+    low[:, :, slots_used:, :] = jnp.zeros((times, bands, spare, low.shape[3]), low.dtype)
+    folded[...] = jnp.zeros_like(folded)
+    for hour in range(2):
+        early = observed_ref[hour, :, :half]
+        late = observed_ref[hour, :, half:]
+        folded[0, hour * ROWS : hour * ROWS + lat_dev, :half] = early + late
+        folded[1, hour * ROWS : hour * ROWS + lat_dev, :half] = early - late
+    rows = []
+    for parity in range(2):
+        upper, lower = split(folded[parity])
+        rows.append((jnp.concatenate([upper, lower], axis=0), upper))
+
+    symmetric_gains(noise_ref, variance_ref[...], scale_ref[...], transition_ref, gain_ref, smoother_ref)
+
+    def flat(ref, time):
+        return ref[time].reshape(bands * width, ref.shape[3])
+
+    for time in range(times):
+        table_copy(time, 0).wait()
+        table_copy(time, 1).wait()
+        both, upper = rows[time % 2]
+        wide = lax.dot_general(both, flat(high, time), NT, preferred_element_type=jnp.float32)
+        rest = lax.dot_general(upper, flat(low, time), NT, preferred_element_type=jnp.float32)
+        spectra = wide[: 2 * ROWS] + wide[2 * ROWS :] + rest
+        for pair in range(bands // 2):
+            block = spectra[:, pair * LANES : (pair + 1) * LANES]
+            outbox[time, 2 * pair], outbox[time, 2 * pair + 1] = swap_halves(block[:ROWS], block[ROWS:])
+
+    pl.semaphore_wait(barrier, devices - 1)
+
+    def exchange(box, landing, sends, recvs, peer, slot):
+        peer_time, peer_band = peer // bands, lax.rem(peer, bands)
+        slot_time, slot_band = slot // bands, lax.rem(slot, bands)
+        return pltpu.make_async_remote_copy(
+            src_ref=box.at[peer_time, peer_band, pl.ds(0, lat_dev)],
+            dst_ref=landing.at[slot_time, slot_band, pl.ds(0, lat_dev)],
+            send_sem=sends.at[peer],
+            recv_sem=recvs.at[slot],
+            device_id=(peer_time, peer_band),
+            device_id_type=MESH,
+        )
+
+    def send(step, carry):
+        peer = lax.rem(me + step, devices)
+        exchange(outbox, inbox, send_sem, recv_sem, peer, me).start()
+        return carry
+
+    def settle(step, carry):
+        peer = lax.rem(me + step, devices)
+        exchange(outbox, inbox, send_sem, recv_sem, peer, peer).wait()
+        return carry
+
+    lax.fori_loop(1, devices, send, 0)
+    inbox[my_time, my_band] = outbox[my_time, my_band]
+    lax.fori_loop(1, devices, settle, 0)
+
+    spectra = []
+    for time in range(times):
+        mixed = lax.dot_general(
+            forward_lat_ref[...],
+            inbox[time].reshape(bands * ROWS, LANES),
+            NN,
+            precision=HIGHEST,
+            preferred_element_type=jnp.float32,
+        )
+        spectra.extend(swap_halves(mixed[:n_half], mixed[n_half:]))
+
+    transition = [[transition_ref[row, column] for column in range(3)] for row in range(3)]
+    means, predictions = [], [None]
+    means.append([gain_ref[0, row] * spectra[0] for row in range(3)])
+    for hour in range(1, hours):
+        predicted = mat_vec(transition, means[-1])
+        residual = spectra[hour] - predicted[0]
+        predictions.append(predicted)
+        means.append([predicted[row] + gain_ref[hour, row] * residual for row in range(3)])
+    smoothed = means[-1]
+    series = [None] * hours
+    series[hours - 1] = smoothed[0]
+    for hour in range(hours - 2, -1, -1):
+        difference = [smoothed[row] - predictions[hour + 1][row] for row in range(3)]
+        smoothed = [
+            means[hour][row]
+            + smoother_ref[hour, row, 0] * difference[0]
+            + smoother_ref[hour, row, 1] * difference[1]
+            + smoother_ref[hour, row, 2] * difference[2]
+            for row in range(3)
+        ]
+        series[hour] = smoothed[0]
+
+    for time in range(times):
+        stacked = jnp.concatenate(swap_halves(series[2 * time], series[2 * time + 1]), axis=0)
+        grid = lax.dot_general(
+            inverse_lat_ref[...], stacked, NN, precision=HIGHEST, preferred_element_type=jnp.float32
+        )
+        outbox_back[time] = grid.reshape(bands, ROWS, LANES)
+
+    def send_back(step, carry):
+        peer = lax.rem(me + step, devices)
+        exchange(outbox_back, inbox_back, send_back_sem, recv_back_sem, peer, me).start()
+        return carry
+
+    def settle_back(step, carry):
+        peer = lax.rem(me + step, devices)
+        exchange(outbox_back, inbox_back, send_back_sem, recv_back_sem, peer, peer).wait()
+        return carry
+
+    lax.fori_loop(1, devices, send_back, 0)
+    inbox_back[my_time, my_band] = outbox_back[my_time, my_band]
+    lax.fori_loop(1, devices, settle_back, 0)
+
+    sums = [None, None]
+    for time in range(times):
+        blocks = []
+        for pair in range(bands // 2):
+            first, second = swap_halves(inbox_back[time, 2 * pair], inbox_back[time, 2 * pair + 1])
+            blocks.append(jnp.concatenate([first, second], axis=0))
+        upper, lower = split(jnp.concatenate(blocks, axis=1))
+        both = jnp.concatenate([upper, lower], axis=0)
+        wide = lax.dot_general(both, flat(high, time), NN, preferred_element_type=jnp.float32)
+        rest = lax.dot_general(upper, flat(low, time), NN, preferred_element_type=jnp.float32)
+        part = wide[: 2 * ROWS] + wide[2 * ROWS :] + rest
+        sums[time % 2] = part if sums[time % 2] is None else sums[time % 2] + part
+    early = sums[0] + sums[1]
+    late = sums[0] - sums[1]
+    for hour in range(2):
+        out_ref[hour, :, :half] = early[hour * ROWS : hour * ROWS + lat_dev, :half]
+        out_ref[hour, :, half:] = late[hour * ROWS : hour * ROWS + lat_dev, :half]
+
+
+def per_device_fused(observed, noise_var, spectral_var, time_scale):
+    times, bands = lax.axis_size("tm"), lax.axis_size("space")
+    hours_dev, lat_dev, lon_size = observed.shape
+    hours, lat_size = noise_var.shape[0], spectral_var.shape[1]
+    slots = spectral_var.shape[0] // times
+    slots_used = round_up(slots, 2 * ROWS)
+    n_half, width = lat_size // 2, LANES // 2
+    half_padded = round_up(lon_size // 2, LANES)
+
+    def own_modes(array):
+        mine = lax.dynamic_index_in_dim(
+            array.reshape(slots, times, lat_size), lax.axis_index("tm"), 1, keepdims=False
+        )
+        mine = jnp.pad(mine.T, ((0, 0), (0, width - slots)), constant_values=1.0)
+        return jnp.concatenate([mine[:n_half], mine[n_half:]], axis=1)
+
+    high, low = lon_tables(lon_size, times, bands, slots_used)
+    forward_lat, inverse_lat = lat_tables(lat_size, bands)
+    in_vmem = pl.BlockSpec(memory_space=pltpu.VMEM)
+    in_place = pl.BlockSpec(memory_space=pl.ANY)
+    box = pltpu.VMEM((times, bands, ROWS, LANES), jnp.float32)
+    table = pltpu.VMEM((times, bands, width, half_padded), jnp.bfloat16)
+    dma = pltpu.SemaphoreType.DMA
+    return pl.pallas_call(
+        functools.partial(smoother_kernel, times, bands, slots_used),
+        out_shape=jax.ShapeDtypeStruct(observed.shape, jnp.float32),
+        in_specs=[in_vmem, pl.BlockSpec(memory_space=pltpu.SMEM)] + [in_vmem] * 4 + [in_place] * 2,
+        out_specs=in_vmem,
+        scratch_shapes=[
+            table,
+            table,
+            pltpu.VMEM((2, 2 * ROWS, half_padded), jnp.float32),
+            box,
+            box,
+            box,
+            box,
+            pltpu.VMEM((3, 3, n_half, LANES), jnp.float32),
+            pltpu.VMEM((hours, 3, n_half, LANES), jnp.float32),
+            pltpu.VMEM((hours, 3, 3, n_half, LANES), jnp.float32),
+            dma((times, 2)),
+            dma((times * bands,)),
+            dma((times * bands,)),
+            dma((times * bands,)),
+            dma((times * bands,)),
+        ],
+        compiler_params=pltpu.CompilerParams(
+            collective_id=0, has_side_effects=True, vmem_limit_bytes=48 * 1024 * 1024
+        ),
+    )(
+        observed,
+        noise_var,
+        own_modes(spectral_var),
+        own_modes(time_scale),
+        jnp.asarray(forward_lat),
+        jnp.asarray(inverse_lat),
+        jnp.asarray(high),
+        jnp.asarray(low),
+    )
+
+
+def fits(observed, spectral_var):
+    times, bands = lax.axis_size("tm"), lax.axis_size("space")
+    hours_dev, lat_dev, lon_size = observed.shape
+    modes_dev, lat_size = spectral_var.shape
+    return (
+        hours_dev == 2
+        and lat_dev <= ROWS
+        and lat_size % (2 * ROWS) == 0
+        and bands % 2 == 0
+        and times % 2 == 0
+        and lon_size % 4 == 0
+        and modes_dev % 2 == 0
+        and modes_dev % times == 0
+        and LANES // 4 < modes_dev // times <= LANES // 2
+    )
+
+
+def per_device(observed, noise_var, spectral_var, time_scale):
+    if fits(observed, spectral_var):
+        return per_device_fused(observed, noise_var, spectral_var, time_scale)
+    return per_device_general(observed, noise_var, spectral_var, time_scale)
+
+
 def solution(mesh):
     placed = (P("tm", "space", None), P(), P("space", None), P("space", None))
     return jax.shard_map(

time: 187 us -> 31.3 us (0.17)
  matrix products: 56.3 us -> 0 us
  other arithmetic: 52 us -> 0.16 us
  local copies, waits for them, and re-layouts: 35.5 us -> 9.15 us
  waiting for transfers between devices: 21.7 us -> 0 us
  Pallas kernels: 0 us -> 21.5 us
  starting transfers between devices: 17.4 us -> 0 us
  loops' own time: 2.67 us -> 0 us
    dot_general x4 -> x0, matrix products: 56.3 us -> none  [the longest x1 46.8 us: per_device(): lax.dot_general(by_band, lon_table, (((0,), (0,)), ((), ())), precision=H...]
    dot_general x1 -> x0, other arithmetic: 39 us -> none  [per_device(): lax.dot_general(lon_table, grid_rows, (((1,), (1,)), ((), ())), precision...]
    dynamic_update_slice x103 -> x0, local copies, waits for them, and re-layouts: 22.2 us -> none  [the longest x96 20.7 us: smooth_series(): lax.scan(forward, ([zeros, zeros, zeros], stationary), (spectra, noise_var))]
    all_to_all x4 -> x0, waiting for transfers between devices: 21.7 us -> none  [the longest x1 7.04 us: per_device(): lax.all_to_all(latitude_grid, 'space', split_axis=1, concat_axis=0, tiled...]
    pallas_call x0 -> x1, Pallas kernels: none -> 21.5 us  [per_device_fused(): pl.pallas_call(functools.partial(smoother_kernel, times, bands, slots_use...]
    all_to_all x4 -> x0, starting transfers between devices: 17.4 us -> none  [the longest x1 7.28 us: per_device(): lax.all_to_all(spectra, 'space', split_axis=0, concat_axis=1, tiled=True)]
    add x63 -> x0, other arithmetic: 7.25 us -> none  [the longest x8 5.31 us: forward(): predicted[across] + kalman_gain[across] * residual]
    dynamic_slice x58 -> x3, local copies, waits for them, and re-layouts: 7.47 us -> 0.22 us  [own_modes(): lax.dynamic_index_in_dim(array.reshape(slots, times, lat_size), lax.axis_...]
  transfers between devices with their start and end apart: 4 -> 0, of which waited for: 4 -> 0; matrix products, arithmetic and copies ran while one was open for 0% -> 0% of each run, Pallas kernels for 0% -> 0%
where the time goes in v1:
time: 31.3 us; the launch traced here: 30.8 us
  Pallas kernels  21.5 us (69%)
  local copies, waits for them, and re-layouts  9.15 us (29%)
    pallas_call x1, Pallas kernels, per_device_fused(): pl.pallas_call(functools.partial(smoother_kernel, times, bands, slots_use...  21.5 us
    unnamed x13, local copies, waits for them, and re-layouts  8.18 us
    pallas_call x1, local copies, waits for them, and re-layouts, per_device_fused(): pl.pallas_call(functools.partial(smoother_kernel, times, bands, slots_use...  0.69 us

profile of v1, /device:TPU:0, one launch (start us, length us, event | category | flops | bytes accessed | tf_op | source)
XLA Modules:
  0.0 30.8 jit_solution(7674588669166373642)
XLA Ops:
  0.0 0.9 %copy.13 = f32[180,48]{1,0:T(8,128)S(1)} copy(f32[180,48]{0,1:T(8,128)} %param.10) | data formatting | bytes 69120 | tf_op args[2]
  0.9 0.9 %copy.15 = f32[180,48]{1,0:T(8,128)S(1)} copy(f32[180,48]{0,1:T(8,128)} %param.11) | data formatting | bytes 69120 | tf_op args[3]
  1.9 0.1 constant_dynamic-slice_fusion
  1.9 0.1 copy.16
  2.0 0.1 pad_maximum_fusion.1.scale_ref
  2.1 0.1 copy.14
  2.2 0.1 pad_maximum_fusion.variance_ref
  2.3 0.9 %copy.17.observed_ref = f32[2,6,1440]{2,1,0:T(8,128)S(1)} copy(f32[2,6,1440]{2,0,1:T(2,128)} %param.8) | data formatting | bytes 138240 | tf_op args[0]
  3.2 0.0 copy-start
  3.2 1.7 %copy-done = bf16[4,8,48,768]{3,2,1,0:T(8,128)(2,1)S(1)} copy-done((bf16[4,8,48,768]{3,2,1,0:T(8,128)(2,1)S(1)}, bf16[4,8,48,768]{3,2,1,0:T(8,128)(2,1)}, u32[]{:S(2)}) %copy-start) | copy-done | bytes 2359320
  4.8 0.0 copy-start.1
  4.8 1.7 %copy-done.1 = bf16[4,8,48,768]{3,2,1,0:T(8,128)(2,1)S(1)} copy-done((bf16[4,8,48,768]{3,2,1,0:T(8,128)(2,1)S(1)}, bf16[4,8,48,768]{3,2,1,0:T(8,128)(2,1)}, u32[]{:S(2)}) %copy-start.1) | copy-done | bytes 2359320
  6.5 0.0 copy-start.2
  6.5 0.8 %copy-done.2 = f32[64,48]{1,0:T(8,128)S(1)} copy-done((f32[64,48]{1,0:T(8,128)S(1)}, f32[64,48]{1,0:T(8,128)}, u32[]{:S(2)}) %copy-start.2) | copy-done | bytes 12312
  7.3 0.0 copy-start.3
  7.3 0.7 %copy-done.3 = f32[48,64]{1,0:T(8,128)S(1)} copy-done((f32[48,64]{1,0:T(8,128)S(1)}, f32[48,64]{1,0:T(8,128)}, u32[]{:S(2)}) %copy-start.3) | copy-done | bytes 12312
  8.0 0.0 copy-start.4
  8.0 0.7 %copy-done.4 = f32[8]{0:T(128)S(1)} copy-done((f32[8]{0:T(128)S(1)}, f32[8]{0:T(128)}, u32[]{:S(2)}) %copy-start.4) | copy-done | bytes 56
  8.7 21.5 %shard_map.82 = f32[2,6,1440]{2,1,0:T(8,128)S(1)} custom-call(f32[2,6,1440]{2,1,0:T(8,128)S(1)} %copy.17.observed_ref, f32[8]{0:T(128)S(1)} %copy-done.4, f32[24,128]{1,0:T(8,128)S(1)} %pad_maximum_fusion.variance_ref, f32[24,128]{1,0:T(8,128)S(1)} %pad_maximum_fusion.1.scale_ref, f32[48,64]{1,0:T(8,128)S(1)} %copy-done.3, f32[64,48]{1,0:T(8,128)S(1)} %copy-done.2, ...), custom_call_target="tpu_custom_call" | custom-call | tf_op jit(solution)/shard_map/pallas_call | solution.py:534
  30.1 0.7 %copy.18 = f32[2,6,1440]{2,0,1:T(2,128)} copy(f32[2,6,1440]{2,1,0:T(8,128)S(1)} %shard_map.82) | data formatting | bytes 138240 | tf_op jit(solution)/shard_map/pallas_call | solution.py:534
  (4 shorter events, 0.1 us)
Async XLA Ops:
  3.2 1.7 %copy-start = (bf16[4,8,48,768]{3,2,1,0:T(8,128)(2,1)S(1)}, bf16[4,8,48,768]{3,2,1,0:T(8,128)(2,1)}, u32[]{:S(2)}) copy-start(bf16[4,8,48,768]{3,2,1,0:T(8,128)(2,1)} %constant.26.clone.low_hbm) | copy-start | bytes 7077892
  4.8 1.7 %copy-start.1 = (bf16[4,8,48,768]{3,2,1,0:T(8,128)(2,1)S(1)}, bf16[4,8,48,768]{3,2,1,0:T(8,128)(2,1)}, u32[]{:S(2)}) copy-start(bf16[4,8,48,768]{3,2,1,0:T(8,128)(2,1)} %constant.25.clone.high_hbm) | copy-start | bytes 7077892
  6.5 0.8 %copy-start.2 = (f32[64,48]{1,0:T(8,128)S(1)}, f32[64,48]{1,0:T(8,128)}, u32[]{:S(2)}) copy-start(f32[64,48]{1,0:T(8,128)} %constant.24.clone.inverse_lat_ref) | copy-start | bytes 36868
  7.3 0.7 %copy-start.3 = (f32[48,64]{1,0:T(8,128)S(1)}, f32[48,64]{1,0:T(8,128)}, u32[]{:S(2)}) copy-start(f32[48,64]{1,0:T(8,128)} %constant.23.clone.forward_lat_ref) | copy-start | bytes 36868
  8.0 0.7 %copy-start.4 = (f32[8]{0:T(128)S(1)}, f32[8]{0:T(128)}, u32[]{:S(2)}) copy-start(f32[8]{0:T(128)} %noise_ref.1) | copy-start | bytes 100

commit v2 on v1

--- a/solution.py
+++ b/solution.py
@@ -318,15 +318,21 @@
     times,
     bands,
     slots_used,
+    observed_hbm,
+    noise_hbm,
+    variance_hbm,
+    scale_hbm,
+    forward_lat_hbm,
+    inverse_lat_hbm,
+    high_hbm,
+    low_hbm,
+    out_ref,
     observed_ref,
     noise_ref,
     variance_ref,
     scale_ref,
     forward_lat_ref,
     inverse_lat_ref,
-    high_hbm,
-    low_hbm,
-    out_ref,
     high,
     low,
     folded,
@@ -337,6 +343,7 @@
     transition_ref,
     gain_ref,
     smoother_ref,
+    input_sem,
     table_sem,
     send_sem,
     recv_sem,
@@ -347,7 +354,7 @@
     my_time = lax.axis_index("tm")
     my_band = lax.axis_index("space")
     me = my_time * bands + my_band
-    lat_dev, lon_size = observed_ref.shape[1], observed_ref.shape[2]
+    lat_dev, lon_size = observed_ref.shape[0], observed_ref.shape[2]
     half = lon_size // 2
     hours = gain_ref.shape[0]
     n_half = gain_ref.shape[2]
@@ -359,9 +366,25 @@
             source.at[time], target.at[time, :, pl.ds(0, slots_used), :], table_sem.at[time, which]
         )
 
+    inputs = [
+        pltpu.make_async_copy(source, target, input_sem.at[index])
+        for index, (source, target) in enumerate(
+            [
+                (observed_hbm, observed_ref),
+                (noise_hbm, noise_ref),
+                (variance_hbm, variance_ref),
+                (scale_hbm, scale_ref),
+                (forward_lat_hbm, forward_lat_ref),
+                (inverse_lat_hbm, inverse_lat_ref),
+            ]
+        )
+    ]
+    inputs[0].start()
     for time in range(times):
         table_copy(time, 0).start()
         table_copy(time, 1).start()
+    for copy in inputs[1:]:
+        copy.start()
 
     inbox[...] = jnp.zeros_like(inbox)
     inbox_back[...] = jnp.zeros_like(inbox_back)
@@ -381,17 +404,16 @@
     high[:, :, slots_used:, :] = jnp.zeros((times, bands, spare, high.shape[3]), high.dtype)
     low[:, :, slots_used:, :] = jnp.zeros((times, bands, spare, low.shape[3]), low.dtype)
     folded[...] = jnp.zeros_like(folded)
+    inputs[0].wait()
     for hour in range(2):
-        early = observed_ref[hour, :, :half]
-        late = observed_ref[hour, :, half:]
+        early = observed_ref[:, hour, :half]
+        late = observed_ref[:, hour, half:]
         folded[0, hour * ROWS : hour * ROWS + lat_dev, :half] = early + late
         folded[1, hour * ROWS : hour * ROWS + lat_dev, :half] = early - late
     rows = []
     for parity in range(2):
         upper, lower = split(folded[parity])
         rows.append((jnp.concatenate([upper, lower], axis=0), upper))
-
-    symmetric_gains(noise_ref, variance_ref[...], scale_ref[...], transition_ref, gain_ref, smoother_ref)
 
     def flat(ref, time):
         return ref[time].reshape(bands * width, ref.shape[3])
@@ -433,6 +455,24 @@
 
     lax.fori_loop(1, devices, send, 0)
     inbox[my_time, my_band] = outbox[my_time, my_band]
+
+    for copy in inputs[1:]:
+        copy.wait()
+    modes_dev = variance_ref.shape[1]
+    slots = modes_dev // times
+    mode = lax.broadcasted_iota(jnp.int32, (modes_dev, LANES), 0)
+    slot = lax.rem(lax.broadcasted_iota(jnp.int32, (modes_dev, LANES), 1), width)
+    picked = ((mode == slot * times + my_time) & (slot < slots)).astype(jnp.float32)
+    tile_lane = lax.broadcasted_iota(jnp.int32, (n_half, LANES), 1)
+
+    def own_modes(ref):
+        mine = lax.dot_general(ref[...], picked, NN, precision=HIGHEST, preferred_element_type=jnp.float32)
+        mine = jnp.where(tile_lane < width, mine[:n_half], mine[n_half:])
+        return jnp.where(lax.rem(tile_lane, width) < slots, mine, 1.0)
+
+    symmetric_gains(
+        noise_ref, own_modes(variance_ref), own_modes(scale_ref), transition_ref, gain_ref, smoother_ref
+    )
     lax.fori_loop(1, devices, settle, 0)
 
     spectra = []
@@ -504,39 +544,37 @@
     early = sums[0] + sums[1]
     late = sums[0] - sums[1]
     for hour in range(2):
-        out_ref[hour, :, :half] = early[hour * ROWS : hour * ROWS + lat_dev, :half]
-        out_ref[hour, :, half:] = late[hour * ROWS : hour * ROWS + lat_dev, :half]
+        out_ref[:, hour, :half] = early[hour * ROWS : hour * ROWS + lat_dev, :half]
+        out_ref[:, hour, half:] = late[hour * ROWS : hour * ROWS + lat_dev, :half]
 
 
 def per_device_fused(observed, noise_var, spectral_var, time_scale):
     times, bands = lax.axis_size("tm"), lax.axis_size("space")
     hours_dev, lat_dev, lon_size = observed.shape
     hours, lat_size = noise_var.shape[0], spectral_var.shape[1]
-    slots = spectral_var.shape[0] // times
-    slots_used = round_up(slots, 2 * ROWS)
+    slots_used = round_up(spectral_var.shape[0] // times, 2 * ROWS)
     n_half, width = lat_size // 2, LANES // 2
     half_padded = round_up(lon_size // 2, LANES)
-
-    def own_modes(array):
-        mine = lax.dynamic_index_in_dim(
-            array.reshape(slots, times, lat_size), lax.axis_index("tm"), 1, keepdims=False
-        )
-        mine = jnp.pad(mine.T, ((0, 0), (0, width - slots)), constant_values=1.0)
-        return jnp.concatenate([mine[:n_half], mine[n_half:]], axis=1)
 
     high, low = lon_tables(lon_size, times, bands, slots_used)
     forward_lat, inverse_lat = lat_tables(lat_size, bands)
     in_vmem = pl.BlockSpec(memory_space=pltpu.VMEM)
-    in_place = pl.BlockSpec(memory_space=pl.ANY)
+    in_place = pl.BlockSpec(memory_space=pltpu.HBM)
     box = pltpu.VMEM((times, bands, ROWS, LANES), jnp.float32)
     table = pltpu.VMEM((times, bands, width, half_padded), jnp.bfloat16)
     dma = pltpu.SemaphoreType.DMA
-    return pl.pallas_call(
+    field = pl.pallas_call(
         functools.partial(smoother_kernel, times, bands, slots_used),
-        out_shape=jax.ShapeDtypeStruct(observed.shape, jnp.float32),
-        in_specs=[in_vmem, pl.BlockSpec(memory_space=pltpu.SMEM)] + [in_vmem] * 4 + [in_place] * 2,
+        out_shape=jax.ShapeDtypeStruct((lat_dev, hours_dev, lon_size), jnp.float32),
+        in_specs=[in_place] * 8,
         out_specs=in_vmem,
         scratch_shapes=[
+            pltpu.VMEM((lat_dev, hours_dev, lon_size), jnp.float32),
+            pltpu.SMEM((hours,), jnp.float32),
+            pltpu.VMEM((lat_size, spectral_var.shape[0]), jnp.float32),
+            pltpu.VMEM((lat_size, spectral_var.shape[0]), jnp.float32),
+            pltpu.VMEM(forward_lat.shape, jnp.float32),
+            pltpu.VMEM(inverse_lat.shape, jnp.float32),
             table,
             table,
             pltpu.VMEM((2, 2 * ROWS, half_padded), jnp.float32),
@@ -547,25 +585,25 @@
             pltpu.VMEM((3, 3, n_half, LANES), jnp.float32),
             pltpu.VMEM((hours, 3, n_half, LANES), jnp.float32),
             pltpu.VMEM((hours, 3, 3, n_half, LANES), jnp.float32),
+            dma((6,)),
             dma((times, 2)),
             dma((times * bands,)),
             dma((times * bands,)),
             dma((times * bands,)),
             dma((times * bands,)),
         ],
-        compiler_params=pltpu.CompilerParams(
-            collective_id=0, has_side_effects=True, vmem_limit_bytes=48 * 1024 * 1024
-        ),
+        compiler_params=pltpu.CompilerParams(collective_id=0, has_side_effects=True),
     )(
-        observed,
+        observed.transpose(1, 0, 2),
         noise_var,
-        own_modes(spectral_var),
-        own_modes(time_scale),
+        spectral_var.T,
+        time_scale.T,
         jnp.asarray(forward_lat),
         jnp.asarray(inverse_lat),
         jnp.asarray(high),
         jnp.asarray(low),
     )
+    return field.transpose(1, 0, 2)
 
 
 def fits(observed, spectral_var):

time: 31.3 us -> 22.9 us (0.73); the launches traced: 30.8 us -> 22.8 us
  local copies, waits for them, and re-layouts: 9.15 us -> 1.52 us
    unnamed x13 -> x1, local copies, waits for them, and re-layouts: 8.18 us -> 1.52 us
    pallas_call x1 -> x0, local copies, waits for them, and re-layouts: 0.69 us -> none  [per_device_fused(): pl.pallas_call(functools.partial(smoother_kernel, times, bands, slots_use...]
where the time goes in v2:
time: 22.9 us; the launch traced here: 22.8 us
  Pallas kernels  21.2 us (93%)
  local copies, waits for them, and re-layouts  1.52 us (7%)
    pallas_call x1, Pallas kernels, per_device_fused(): pl.pallas_call(functools.partial(smoother_kernel, times, bands, slots_use...  21.2 us
    unnamed x1, local copies, waits for them, and re-layouts  1.52 us

profile of v2, /device:TPU:0, one launch (start us, length us, event | category | flops | bytes accessed | tf_op | source)
XLA Modules:
  0.0 22.8 jit_solution(1091026417637566033)
XLA Ops:
  0.0 21.2 %shard_map.82 = f32[6,2,1440]{2,1,0:T(2,128)} custom-call(f32[6,2,1440]{2,1,0:T(2,128)} %bitcast.5, f32[8]{0:T(128)} %noise_hbm.1, f32[48,180]{1,0:T(8,128)} %bitcast.6, f32[48,180]{1,0:T(8,128)} %bitcast.7, f32[48,64]{1,0:T(8,128)} %constant.8.clone.forward_lat_hbm, f32[64,48]{1,0:T(8,128)} %constant.9.clone.inverse_lat_hbm, ...), custom_call_target="tpu_custom_call" | custom-call | tf_op jit(solution)/shard_map/pallas_call | solution.py:566
  21.3 1.5 %copy.10 = f32[2,6,1440]{2,0,1:T(2,128)} copy(f32[2,6,1440]{2,0,1:T(2,128)} %bitcast.4) | data formatting | bytes 138240

commit v3 on v2

--- a/solution.py
+++ b/solution.py
@@ -242,13 +242,25 @@
     full = np.zeros((lat_size, bands, ROWS), np.float32)
     full[:, :, :lat_dev] = table.reshape(lat_size, bands, lat_dev)
     full = full.reshape(lat_size, bands * ROWS)
-    return full, np.ascontiguousarray(full.T)
+
+    def stacked(array):
+        high = array.astype(jnp.bfloat16)
+        return np.concatenate([high, (array - high.astype(np.float32)).astype(jnp.bfloat16)], axis=0)
+
+    return stacked(full), stacked(np.ascontiguousarray(full.T))
 
 
 def split(value):
     high = value.astype(jnp.bfloat16)
     low = (value - high.astype(jnp.float32)).astype(jnp.bfloat16)
     return high, low
+
+
+def paired_dot(table, value):
+    both = jnp.concatenate(split(value), axis=1)
+    product = lax.dot_general(table, both, NN, preferred_element_type=jnp.float32)
+    rows = table.shape[0] // 2
+    return product[:rows, :LANES] + (product[:rows, LANES:] + product[rows:, :LANES])
 
 
 def swap_halves(first, second):
@@ -427,19 +439,18 @@
         spectra = wide[: 2 * ROWS] + wide[2 * ROWS :] + rest
         for pair in range(bands // 2):
             block = spectra[:, pair * LANES : (pair + 1) * LANES]
-            outbox[time, 2 * pair], outbox[time, 2 * pair + 1] = swap_halves(block[:ROWS], block[ROWS:])
+            owner = time * bands + 2 * pair
+            outbox[owner], outbox[owner + 1] = swap_halves(block[:ROWS], block[ROWS:])
 
     pl.semaphore_wait(barrier, devices - 1)
 
     def exchange(box, landing, sends, recvs, peer, slot):
-        peer_time, peer_band = peer // bands, lax.rem(peer, bands)
-        slot_time, slot_band = slot // bands, lax.rem(slot, bands)
         return pltpu.make_async_remote_copy(
-            src_ref=box.at[peer_time, peer_band, pl.ds(0, lat_dev)],
-            dst_ref=landing.at[slot_time, slot_band, pl.ds(0, lat_dev)],
-            send_sem=sends.at[peer],
-            recv_sem=recvs.at[slot],
-            device_id=(peer_time, peer_band),
+            src_ref=box.at[peer, pl.ds(0, lat_dev)],
+            dst_ref=landing.at[slot, pl.ds(0, lat_dev)],
+            send_sem=sends.at[0],
+            recv_sem=recvs.at[slot // bands],
+            device_id=(peer // bands, lax.rem(peer, bands)),
             device_id_type=MESH,
         )
 
@@ -448,13 +459,18 @@
         exchange(outbox, inbox, send_sem, recv_sem, peer, me).start()
         return carry
 
-    def settle(step, carry):
-        peer = lax.rem(me + step, devices)
-        exchange(outbox, inbox, send_sem, recv_sem, peer, peer).wait()
-        return carry
+    def sent(box, sends):
+        gone = box.at[pl.ds(0, devices - 1), pl.ds(0, lat_dev)]
+        pltpu.make_async_copy(gone, gone, sends.at[0]).wait()
+
+    def arrive(landing, recvs, step):
+        time = lax.rem(my_time + step, times)
+        come = landing.at[pl.ds(0, bands - 1 if step == 0 else bands), pl.ds(0, lat_dev)]
+        pltpu.make_async_copy(come, come, recvs.at[time]).wait()
+        return time
 
     lax.fori_loop(1, devices, send, 0)
-    inbox[my_time, my_band] = outbox[my_time, my_band]
+    inbox[me] = outbox[me]
 
     for copy in inputs[1:]:
         copy.wait()
@@ -473,17 +489,14 @@
     symmetric_gains(
         noise_ref, own_modes(variance_ref), own_modes(scale_ref), transition_ref, gain_ref, smoother_ref
     )
-    lax.fori_loop(1, devices, settle, 0)
+    sent(outbox, send_sem)
+    for step in range(times):
+        arrive(inbox, recv_sem, step)
 
     spectra = []
     for time in range(times):
-        mixed = lax.dot_general(
-            forward_lat_ref[...],
-            inbox[time].reshape(bands * ROWS, LANES),
-            NN,
-            precision=HIGHEST,
-            preferred_element_type=jnp.float32,
-        )
+        arrived = inbox[time * bands : (time + 1) * bands].reshape(bands * ROWS, LANES)
+        mixed = paired_dot(forward_lat_ref[...], arrived)
         spectra.extend(swap_halves(mixed[:n_half], mixed[n_half:]))
 
     transition = [[transition_ref[row, column] for column in range(3)] for row in range(3)]
@@ -510,39 +523,33 @@
 
     for time in range(times):
         stacked = jnp.concatenate(swap_halves(series[2 * time], series[2 * time + 1]), axis=0)
-        grid = lax.dot_general(
-            inverse_lat_ref[...], stacked, NN, precision=HIGHEST, preferred_element_type=jnp.float32
-        )
-        outbox_back[time] = grid.reshape(bands, ROWS, LANES)
+        grid = paired_dot(inverse_lat_ref[...], stacked)
+        outbox_back[time * bands : (time + 1) * bands] = grid.reshape(bands, ROWS, LANES)
 
     def send_back(step, carry):
         peer = lax.rem(me + step, devices)
         exchange(outbox_back, inbox_back, send_back_sem, recv_back_sem, peer, me).start()
         return carry
 
-    def settle_back(step, carry):
-        peer = lax.rem(me + step, devices)
-        exchange(outbox_back, inbox_back, send_back_sem, recv_back_sem, peer, peer).wait()
-        return carry
-
     lax.fori_loop(1, devices, send_back, 0)
-    inbox_back[my_time, my_band] = outbox_back[my_time, my_band]
-    lax.fori_loop(1, devices, settle_back, 0)
-
-    sums = [None, None]
-    for time in range(times):
+    inbox_back[me] = outbox_back[me]
+
+    early = late = 0.0
+    for step in range(times):
+        time = arrive(inbox_back, recv_back_sem, step)
         blocks = []
         for pair in range(bands // 2):
-            first, second = swap_halves(inbox_back[time, 2 * pair], inbox_back[time, 2 * pair + 1])
+            owner = time * bands + 2 * pair
+            first, second = swap_halves(inbox_back[owner], inbox_back[owner + 1])
             blocks.append(jnp.concatenate([first, second], axis=0))
         upper, lower = split(jnp.concatenate(blocks, axis=1))
         both = jnp.concatenate([upper, lower], axis=0)
         wide = lax.dot_general(both, flat(high, time), NN, preferred_element_type=jnp.float32)
         rest = lax.dot_general(upper, flat(low, time), NN, preferred_element_type=jnp.float32)
         part = wide[: 2 * ROWS] + wide[2 * ROWS :] + rest
-        sums[time % 2] = part if sums[time % 2] is None else sums[time % 2] + part
-    early = sums[0] + sums[1]
-    late = sums[0] - sums[1]
+        early = early + part
+        late = late + jnp.where(lax.rem(time, 2) == 0, part, -part)
+    sent(outbox_back, send_back_sem)
     for hour in range(2):
         out_ref[:, hour, :half] = early[hour * ROWS : hour * ROWS + lat_dev, :half]
         out_ref[:, hour, half:] = late[hour * ROWS : hour * ROWS + lat_dev, :half]
@@ -560,12 +567,12 @@
     forward_lat, inverse_lat = lat_tables(lat_size, bands)
     in_vmem = pl.BlockSpec(memory_space=pltpu.VMEM)
     in_place = pl.BlockSpec(memory_space=pltpu.HBM)
-    box = pltpu.VMEM((times, bands, ROWS, LANES), jnp.float32)
+    box = pltpu.VMEM((times * bands, ROWS, LANES), jnp.float32)
     table = pltpu.VMEM((times, bands, width, half_padded), jnp.bfloat16)
     dma = pltpu.SemaphoreType.DMA
     field = pl.pallas_call(
         functools.partial(smoother_kernel, times, bands, slots_used),
-        out_shape=jax.ShapeDtypeStruct((lat_dev, hours_dev, lon_size), jnp.float32),
+        out_shape=pltpu.VMEM((lat_dev, hours_dev, lon_size), jnp.float32),
         in_specs=[in_place] * 8,
         out_specs=in_vmem,
         scratch_shapes=[
@@ -573,8 +580,8 @@
             pltpu.SMEM((hours,), jnp.float32),
             pltpu.VMEM((lat_size, spectral_var.shape[0]), jnp.float32),
             pltpu.VMEM((lat_size, spectral_var.shape[0]), jnp.float32),
-            pltpu.VMEM(forward_lat.shape, jnp.float32),
-            pltpu.VMEM(inverse_lat.shape, jnp.float32),
+            pltpu.VMEM(forward_lat.shape, jnp.bfloat16),
+            pltpu.VMEM(inverse_lat.shape, jnp.bfloat16),
             table,
             table,
             pltpu.VMEM((2, 2 * ROWS, half_padded), jnp.float32),
@@ -587,10 +594,10 @@
             pltpu.VMEM((hours, 3, 3, n_half, LANES), jnp.float32),
             dma((6,)),
             dma((times, 2)),
-            dma((times * bands,)),
-            dma((times * bands,)),
-            dma((times * bands,)),
-            dma((times * bands,)),
+            dma((1,)),
+            dma((times,)),
+            dma((1,)),
+            dma((times,)),
         ],
         compiler_params=pltpu.CompilerParams(collective_id=0, has_side_effects=True),
     )(

time: 22.9 us -> 20.3 us (0.89)
  Pallas kernels: 21.2 us -> 19.5 us
  local copies, waits for them, and re-layouts: 1.52 us -> 0.64 us
    pallas_call x1, Pallas kernels: 21.2 us -> 19.5 us  [per_device_fused(): pl.pallas_call(functools.partial(smoother_kernel, times, bands, slots_use...]
    unnamed x1, local copies, waits for them, and re-layouts: 1.52 us -> 0.64 us
where the time goes in v3:
time: 20.3 us; the launch traced here: 20.1 us
  Pallas kernels  19.5 us (96%)
  local copies, waits for them, and re-layouts  0.64 us (3%)
    pallas_call x1, Pallas kernels, per_device_fused(): pl.pallas_call(functools.partial(smoother_kernel, times, bands, slots_use...  19.5 us
    unnamed x1, local copies, waits for them, and re-layouts  0.64 us

profile of v3, /device:TPU:0, one launch (start us, length us, event | category | flops | bytes accessed | tf_op | source)
XLA Modules:
  0.0 20.1 jit_solution(7958249084598392529)
XLA Ops:
  0.0 19.5 %shard_map.82 = f32[6,2,1440]{2,1,0:T(2,128)S(1)} custom-call(f32[6,2,1440]{2,1,0:T(2,128)} %bitcast.5, f32[8]{0:T(128)} %noise_hbm.1, f32[48,180]{1,0:T(8,128)} %bitcast.6, f32[48,180]{1,0:T(8,128)} %bitcast.7, bf16[96,64]{1,0:T(8,128)(2,1)} %constant.8.clone.forward_lat_hbm, bf16[128,48]{1,0:T(8,128)(2,1)} %constant.9.clone.inverse_lat_hbm, ...), custom_call_target="tpu_custom_call" | custom-call | tf_op jit(solution)/shard_map/pallas_call | solution.py:573
  19.5 0.6 %copy.10 = f32[2,6,1440]{2,0,1:T(2,128)} copy(f32[2,6,1440]{2,0,1:T(2,128)S(1)} %bitcast.4) | data formatting | bytes 138240

commit v4 on v3

--- a/solution.py
+++ b/solution.py
@@ -363,6 +363,7 @@
     recv_back_sem,
 ):
     devices = times * bands
+    stride = 5 if devices % 5 else 1
     my_time = lax.axis_index("tm")
     my_band = lax.axis_index("space")
     me = my_time * bands + my_band
@@ -455,7 +456,7 @@
         )
 
     def send(step, carry):
-        peer = lax.rem(me + step, devices)
+        peer = lax.rem(me + step * stride, devices)
         exchange(outbox, inbox, send_sem, recv_sem, peer, me).start()
         return carry
 
@@ -489,7 +490,6 @@
     symmetric_gains(
         noise_ref, own_modes(variance_ref), own_modes(scale_ref), transition_ref, gain_ref, smoother_ref
     )
-    sent(outbox, send_sem)
     for step in range(times):
         arrive(inbox, recv_sem, step)
 
@@ -527,7 +527,7 @@
         outbox_back[time * bands : (time + 1) * bands] = grid.reshape(bands, ROWS, LANES)
 
     def send_back(step, carry):
-        peer = lax.rem(me + step, devices)
+        peer = lax.rem(me + step * stride, devices)
         exchange(outbox_back, inbox_back, send_back_sem, recv_back_sem, peer, me).start()
         return carry
 
@@ -549,6 +549,7 @@
         part = wide[: 2 * ROWS] + wide[2 * ROWS :] + rest
         early = early + part
         late = late + jnp.where(lax.rem(time, 2) == 0, part, -part)
+    sent(outbox, send_sem)
     sent(outbox_back, send_back_sem)
     for hour in range(2):
         out_ref[:, hour, :half] = early[hour * ROWS : hour * ROWS + lat_dev, :half]

time: 20.3 us -> 19.9 us (0.980)
  Pallas kernels: 19.5 us -> 19 us
    pallas_call x1, Pallas kernels: 19.5 us -> 19 us  [per_device_fused(): pl.pallas_call(functools.partial(smoother_kernel, times, bands, slots_use...]
where the time goes in v4:
time: 19.9 us; the launch traced here: 19.7 us
  Pallas kernels  19 us (95%)
  local copies, waits for them, and re-layouts  0.64 us (3%)
    pallas_call x1, Pallas kernels, per_device_fused(): pl.pallas_call(functools.partial(smoother_kernel, times, bands, slots_use...  19 us
    unnamed x1, local copies, waits for them, and re-layouts  0.64 us

profile of v4, /device:TPU:0, one launch (start us, length us, event | category | flops | bytes accessed | tf_op | source)
XLA Modules:
  0.0 19.7 jit_solution(1372688835925970417)
XLA Ops:
  0.0 19.0 %shard_map.82 = f32[6,2,1440]{2,1,0:T(2,128)S(1)} custom-call(f32[6,2,1440]{2,1,0:T(2,128)} %bitcast.5, f32[8]{0:T(128)} %noise_hbm.1, f32[48,180]{1,0:T(8,128)} %bitcast.6, f32[48,180]{1,0:T(8,128)} %bitcast.7, bf16[96,64]{1,0:T(8,128)(2,1)} %constant.8.clone.forward_lat_hbm, bf16[128,48]{1,0:T(8,128)(2,1)} %constant.9.clone.inverse_lat_hbm, ...), custom_call_target="tpu_custom_call" | custom-call | tf_op jit(solution)/shard_map/pallas_call | solution.py:574
  19.1 0.6 %copy.10 = f32[2,6,1440]{2,0,1:T(2,128)} copy(f32[2,6,1440]{2,0,1:T(2,128)S(1)} %bitcast.4) | data formatting | bytes 138240
